TPU v7x, 512 devices: a whole 4x8x8 slice. The times are simulated.
512 devices in a mesh: sib: 8 (over z_hi, x), leaf: 64 (over y, z_lo, core).
Axes of the slice: x: 4, y: 8, z: 8 (z_hi: 2, z_lo: 4; z = z_hi * 4 + z_lo), core: 2. Of those that a mesh axis runs over, the one named last changes fastest.
Arguments:
- t_int: float32 [64, 512, 1024], P('leaf', 'sib'), as said below
- t_ext: float32 [64, 512, 512], P('leaf', 'sib'), may hold values from -6 to 6
- iface_map: int32 [64, 512], P('leaf'), may hold values from 0 to 511, each once within a row
Outputs:
- own_map: float32 [64, 512, 512], P('leaf', 'sib')
- cross_map: float32 [64, 512, 512], P('leaf', 'sib')
- solution_op: float32 [64, 512, 512], P('leaf', 'sib')
Inputs may be any that keep to these rules, and one draw needn't show every extreme that they name: For each box, the last 512 columns of t_int form a symmetric matrix equal to the identity plus a positive semidefinite matrix. `iface_map`: each row is a permutation of 0 to 511.
All inputs are finite; a program needn't handle non-finite values.
Results may differ from a plain program's by a relative error of at most 0.0003.
Values sent between devices are 32-bit elements; how exact they have to be, the bound alone decides.
A program may use at most 64 MiB of HBM per device.

v0:
```python
import jax
import jax.numpy as jnp
from jax import lax
from jax.sharding import PartitionSpec as P


def partner_2(shard, axis, distance):
    return lax.ppermute(shard, axis, [(i, i ^ 1 << distance) for i in range(lax.axis_size(axis))])


def side_by_side(arrays, axis, dim, along):
    ends, at = ([], 0)
    for a in arrays[:-1]:
        at += a.shape[along]
        ends.append(at)
    both = jnp.concatenate(arrays, axis=along)
    return tuple(jnp.split(lax.all_gather(both, axis, axis=dim, tiled=True), ends, axis=along))


def common_order(matrix, index_map):
    points = index_map.shape[0]
    inverse = jnp.zeros((points,), jnp.int32).at[index_map].set(jnp.arange(points, dtype=jnp.int32))
    picked = matrix[inverse]
    outer_width = matrix.shape[1] - points
    return (picked[:, :outer_width], picked[:, outer_width + inverse])


def lower_solve(factor, right_side, flipped):
    return lax.linalg.triangular_solve(
        factor, right_side, left_side=True, lower=True, transpose_a=flipped
    )


def batch_product(left, right):
    return jnp.einsum(
        "bki,bkj->bij",
        left,
        right,
        precision=lax.Precision.HIGHEST,
        preferred_element_type=jnp.float32,
    )


def on_device(t_int, t_ext, iface_map):
    shard_rows = t_ext.shape[1]
    first_row = lax.axis_index("sib") * shard_rows
    top_bit = lax.axis_size("leaf").bit_length() - 2
    near_rows, other_map = partner_2((t_int, iface_map), "leaf", top_bit)
    own_rows, other_rows = side_by_side((t_int, near_rows), "sib", 1, 0)
    own_outer, own_iface = jax.vmap(common_order)(own_rows, iface_map)
    other_outer, other_iface = jax.vmap(common_order)(other_rows, other_map)
    factor = jnp.linalg.cholesky(own_iface + other_iface)
    solved = lower_solve(factor, own_outer, False)
    partner = lower_solve(factor, other_outer, False)
    solved_block = lax.dynamic_slice_in_dim(solved, first_row, shard_rows, 2)
    own_map = t_ext - batch_product(solved_block, solved)
    cross_map = -batch_product(solved_block, partner)
    back_solved = lower_solve(factor, solved, True)
    solution_op = -lax.dynamic_slice_in_dim(back_solved, first_row, shard_rows, 1)
    return (own_map, cross_map, solution_op)


def solution(mesh):
    placed = (P("leaf", "sib", None), P("leaf", "sib", None), P("leaf", None))
    return jax.shard_map(
        on_device,
        mesh=mesh,
        in_specs=placed,
        out_specs=(P("leaf", "sib", None), P("leaf", "sib", None), P("leaf", "sib", None)),
        check_vma=False,
    )
```

profile of v0, /device:TPU:56, one launch (start us, length us, event | category | flops | bytes accessed | tf_op | source)
XLA Modules:
  0.0 352.2 jit_solution(8187183475571922265)
XLA Ops:
  7.2 4.7 %collective-permute-start = (f32[1,64,1024]{2,1,0:T(8,128)}, f32[1,64,1024]{2,1,0:T(8,128)S(1)}, u32[]{:S(2)}, u32[]{:S(2)}) collective-permute-start(f32[1,64,1024]{2,1,0:T(8,128)} %param.5), channel_id=1, source_target_pairs={{0,32},{1,33},{2,34},{3,35},{4,36},{5,37},{6,38},{7,39},{8,40},{9,... | collective-permute-start | bytes 786440 | tf_op jit(solution)/shard_map/ppermute | solution.py:8
  11.9 15.0 %collective-permute-done = f32[1,64,1024]{2,1,0:T(8,128)S(1)} collective-permute-done((f32[1,64,1024]{2,1,0:T(8,128)}, f32[1,64,1024]{2,1,0:T(8,128)S(1)}, u32[]{:S(2)}, u32[]{:S(2)}) %collective-permute-start) | collective-permute-done | bytes 262176 | tf_op jit(solution)/shard_map/ppermute | solution.py:8
  28.7 3.9 %collective-permute-start.1 = (s32[1,512]{1,0:T(1,128)}, s32[1,512]{1,0:T(1,128)S(1)}, u32[]{:S(2)}, u32[]{:S(2)}) collective-permute-start(s32[1,512]{1,0:T(1,128)} %param.7), channel_id=1, source_target_pairs={{0,32},{1,33},{2,34},{3,35},{4,36},{5,37},{6,38},{7,39},{8,40},{9,... | collective-permute-start | bytes 6152 | tf_op jit(solution)/shard_map/ppermute | solution.py:8
  33.4 5.0 %collective-permute-done.1 = s32[1,512]{1,0:T(1,128)S(1)} collective-permute-done((s32[1,512]{1,0:T(1,128)}, s32[1,512]{1,0:T(1,128)S(1)}, u32[]{:S(2)}, u32[]{:S(2)}) %collective-permute-start.1) | collective-permute-done | bytes 2080 | tf_op jit(solution)/shard_map/ppermute | solution.py:8
  43.4 102.3 %all-gather.2.cloned.1.call-done = f32[2,512,1024]{2,1,0:T(8,128)} async-done(((f32[2,64,1024]{2,1,0:T(8,128)}), f32[2,512,1024]{2,1,0:T(8,128)}) %all-gather.2.cloned.1.call-update) | async-done | bytes 4194320 | tf_op jit(solution)/shard_map/all_gather | solution.py:17
  145.7 4.1 %fusion.99 = (f32[1,512,1024]{2,1,0:T(8,128)S(1)}, f32[1,512,1024]{2,1,0:T(8,128)}) fusion(f32[2,512,1024]{2,1,0:T(8,128)} %all-gather.2.cloned.1.call-done), kind=kLoop, calls=%fused_computation.207 | loop fusion | bytes 8388608 | tf_op jit(solution)/shard_map/split | solution.py:17
  149.8 10.1 %gather_fusion = f32[512,1024]{1,0:T(8,128)} fusion(f32[1,512,1024]{2,1,0:T(8,128)} %get-tuple-element.39, s32[512]{0:T(512)S(1)} %bitcast.325), kind=kCustom, calls=%fused_computation | custom fusion | bytes 4198400 | tf_op jit(solution)/shard_map/vmap()/gather | solution.py:23
  159.9 2.9 copy.9
  162.8 6.6 %gather_fusion.2 = f32[512,1024]{1,0:T(8,128)} fusion(f32[1,512,1024]{2,1,0:T(8,128)S(1)} %get-tuple-element.38, s32[512]{0:T(512)S(1)} %bitcast.324), kind=kCustom, calls=%fused_computation.2 | custom fusion | bytes 4198400 | tf_op jit(solution)/shard_map/vmap()/gather | solution.py:23
  169.5 3.1 copy.10
  172.5 2.9 gather_fusion.1
  175.4 6.4 %gather_fusion.3 = f32[512,512]{1,0:T(8,128)S(1)} fusion(f32[1,512,1024]{1,2,0:T(8,128)} %copy.10, s32[512]{0:T(512)S(1)} %bitcast.327), kind=kCustom, calls=%fused_computation.3 | custom fusion | bytes 2101248 | tf_op jit(solution)/shard_map/vmap()/gather | solution.py:25
  185.0 11.7 %custom-call.37 = f32[1,128,128]{2,1,0:T(8,128)S(1)} custom-call(f32[1,128,128]{2,1,0:T(8,128)S(1)} %cholesky.267), custom_call_target="Cholesky" | custom-call | tf_op jit(solution)/shard_map/jit(cholesky)/cholesky | solution.py:52
  196.8 9.8 %custom-call.38 = f32[1,1,128,128]{2,3,1,0:T(8,128)S(1)} custom-call(f32[1,1,128,128]{3,2,1,0:T(8,128)S(1)} %get-tuple-element.49), custom_call_target="InvertDiagBlocksLowerTriangular" | custom-call | tf_op jit(solution)/shard_map/jit(cholesky)/cholesky | solution.py:52
  209.2 11.7 %custom-call.39 = f32[1,128,128]{2,1,0:T(8,128)S(1)} custom-call(f32[1,128,128]{2,1,0:T(8,128)S(1)} %cholesky.271), custom_call_target="Cholesky" | custom-call | tf_op jit(solution)/shard_map/jit(cholesky)/cholesky | solution.py:52
  220.9 10.0 %custom-call.40 = f32[1,1,128,128]{2,3,1,0:T(8,128)S(1)} custom-call(f32[1,1,128,128]{3,2,1,0:T(8,128)S(1)} %get-tuple-element.46), custom_call_target="InvertDiagBlocksLowerTriangular" | custom-call | tf_op jit(solution)/shard_map/jit(cholesky)/cholesky | solution.py:52
  232.5 11.7 %custom-call.41 = f32[1,128,128]{2,1,0:T(8,128)S(1)} custom-call(f32[1,128,128]{2,1,0:T(8,128)S(1)} %cholesky.276), custom_call_target="Cholesky" | custom-call | tf_op jit(solution)/shard_map/jit(cholesky)/cholesky | solution.py:52
  244.2 9.8 %custom-call.42 = f32[1,1,128,128]{2,3,1,0:T(8,128)S(1)} custom-call(f32[1,1,128,128]{3,2,1,0:T(8,128)S(1)} %get-tuple-element.43), custom_call_target="InvertDiagBlocksLowerTriangular" | custom-call | tf_op jit(solution)/shard_map/jit(cholesky)/cholesky | solution.py:52
  255.6 11.9 %custom-call.43 = f32[1,128,128]{2,1,0:T(8,128)S(1)} custom-call(f32[1,128,128]{2,1,0:T(8,128)S(1)} %fusion.24), custom_call_target="Cholesky" | custom-call | tf_op jit(solution)/shard_map/jit(cholesky)/cholesky | solution.py:52
  273.8 14.0 %while.5 = (s32[]{:T(128)}, f32[1,512,512]{2,1,0:T(8,128)}, s32[4,2]{0,1:T(2,128)S(1)}, f32[4,1,128,128]{3,2,1,0:T(8,128)}, s32[]{:T(128)}) while((s32[]{:T(128)}, f32[1,512,512]{2,1,0:T(8,128)}, s32[4,2]{0,1:T(2,128)S(1)}, f32[4,1,128,128]{3,2,1,0:T(8,128)}, s32[]{:T(128)}) %tuple.42), condition=%wide.while_cond, body=%wide.while_body.sunk | while | flops 2 | bytes 132205 | solution.py:29
  274.4 2.9 bitcast_dynamic-update-slice_fusion.2
  277.9 2.9 bitcast_dynamic-update-slice_fusion.2
  281.4 2.9 bitcast_dynamic-update-slice_fusion.2
  287.8 40.2 %custom-call.54 = f32[1,4,128,128]{2,3,1,0:T(8,128)S(1)} custom-call(f32[1,4,128,128]{3,2,1,0:T(8,128)} %bitcast.353), custom_call_target="InvertDiagBlocksLowerTriangular" | custom-call | tf_op jit(solution)/shard_map/triangular_solve/custom-call.3 | solution.py:29
  (91 shorter events, 42.1 us)
Async XLA Ops:
  7.2 138.5 %all-gather.2.cloned.1.call-start = ((), (), s32[]{:S(2)}) async-start(), calls=%async_computation | async-start | bytes 4718592 | tf_op jit(solution)/shard_map/all_gather | solution.py:17
  7.2 19.7 %collective-permute-start = (f32[1,64,1024]{2,1,0:T(8,128)}, f32[1,64,1024]{2,1,0:T(8,128)S(1)}, u32[]{:S(2)}, u32[]{:S(2)}) collective-permute-start(f32[1,64,1024]{2,1,0:T(8,128)} %param.5), channel_id=1, source_target_pairs={{0,32},{1,33},{2,34},{3,35},{4,36},{5,37},{6,38},{7,39},{8,40},{9,... | collective-permute-start | bytes 786440 | tf_op jit(solution)/shard_map/ppermute | solution.py:8
  28.7 9.6 %collective-permute-start.1 = (s32[1,512]{1,0:T(1,128)}, s32[1,512]{1,0:T(1,128)S(1)}, u32[]{:S(2)}, u32[]{:S(2)}) collective-permute-start(s32[1,512]{1,0:T(1,128)} %param.7), channel_id=1, source_target_pairs={{0,32},{1,33},{2,34},{3,35},{4,36},{5,37},{6,38},{7,39},{8,40},{9,... | collective-permute-start | bytes 6152 | tf_op jit(solution)/shard_map/ppermute | solution.py:8
  169.5 3.1 copy-start
  184.9 11.7 %copy-start.3 = (f32[1,512,512]{2,1,0:T(8,128)}, f32[1,512,512]{2,1,0:T(8,128)S(1)}, u32[]{:S(2)}) copy-start(f32[1,512,512]{2,1,0:T(8,128)S(1)} %fusion.31) | copy-start | bytes 3145732
  254.1 75.3 %copy-start.1 = (f32[512,1024]{1,0:T(8,128)S(1)}, f32[512,1024]{1,0:T(8,128)}, u32[]{:S(2)}) copy-start(f32[512,1024]{1,0:T(8,128)} %gather_fusion.2) | copy-start | bytes 6291460
  287.8 43.8 %copy-start.2 = (f32[1,512,512]{2,1,0:T(8,128)S(1)}, f32[1,512,512]{2,1,0:T(8,128)}, u32[]{:S(2)}) copy-start(f32[1,512,512]{2,1,0:T(8,128)} %get-tuple-element.103) | copy-start | bytes 3145732
  336.3 2.4 copy-start.4
Sparse Core Ops, SparseCore 0:
  28.9 116.7 all-gather.1
where the time goes:
time: 359 us; the launch traced here: 352 us
  other arithmetic  126 us (35%)
  waiting for transfers between devices  122 us (34%)
  local copies, waits for them, and re-layouts  56.5 us (16%)
  matrix products  21.5 us (6%)
  between operations  17.5 us (5%)
  starting transfers between devices  8.66 us (2%)
    all_gather x1, waiting for transfers between devices, side_by_side(): lax.all_gather(both, axis, axis=dim, tiled=True)  102 us
    another operation x15, other arithmetic, on_device(): factor = jnp.linalg.cholesky(own_iface + other_iface)  79.4 us
    another operation x5, other arithmetic, lower_solve(): lax.linalg.triangular_solve(factor, right_side, left_side=True, lower=Tru...  41.4 us
    gather x6, local copies, waits for them, and re-layouts, common_order(): picked = matrix[inverse]  22.7 us
    ppermute x2, waiting for transfers between devices, partner_2(): lax.ppermute(shard, axis, [(i, i ^ 1 << distance) for i in range(lax.axis...  20 us
    another operation x13, local copies, waits for them, and re-layouts, lower_solve(): lax.linalg.triangular_solve(factor, right_side, left_side=True, lower=Tru...  14 us
    another operation x21, matrix products, lower_solve(): lax.linalg.triangular_solve(factor, right_side, left_side=True, lower=Tru...  13.1 us
    gather x4, local copies, waits for them, and re-layouts, common_order(): return (picked[:, :outer_width], picked[:, outer_width + inverse])  9.29 us
  transfers between devices with their start and end apart: 3, of which 3 were waited for; matrix products, arithmetic and copies ran while one was open for 2% of the time, Pallas kernels for 0%

commit v1 on v0

v1 whole, which is shorter than its diff:
```python
import jax
import jax.numpy as jnp
from jax import lax
from jax.experimental import pallas as pl
from jax.experimental.pallas import tpu as pltpu
from jax.sharding import PartitionSpec as P

MESH = pl.DeviceIdType.MESH
POINTS = 512
ROWS = 64
HALF = 32
BLOCK = 128
XR, XL, RR, RL, Y, Z, YC, ZC = 0, 8, 16, 20, 24, 26, 28, 29
COPIES = 30


def matmul(a, b, dims=((1,), (0,))):
    return lax.dot_general(a, b, (dims, ((), ())), preferred_element_type=jnp.float32)


def exact_matmul(a, b):
    return jnp.dot(a, b, precision=lax.Precision.HIGHEST, preferred_element_type=jnp.float32)


def thirds(x):
    high = x.astype(jnp.bfloat16)
    rest = x - high.astype(jnp.float32)
    mid = rest.astype(jnp.bfloat16)
    low = (rest - mid.astype(jnp.float32)).astype(jnp.bfloat16)
    return high, mid, low


def halves(x):
    high = x.astype(jnp.bfloat16)
    return high, (x - high.astype(jnp.float32)).astype(jnp.bfloat16)


def select_rows(onehot, x):
    high, mid, low = thirds(x)
    return matmul(onehot, high) + (matmul(onehot, mid) + matmul(onehot, low))


def select_columns(x, onehot, dims):
    high, mid, low = thirds(x)
    return matmul(high, onehot, dims) + (matmul(mid, onehot, dims) + matmul(low, onehot, dims))


def product(a, b):
    a_high, a_low = halves(a)
    b_high, b_low = halves(b)
    return matmul(a_high, b_high) + (matmul(a_high, b_low) + matmul(a_low, b_high))


def block_inverse(strips):
    lane = lax.broadcasted_iota(jnp.int32, (8, BLOCK), 1)
    sub = lax.broadcasted_iota(jnp.int32, (8, BLOCK), 0)
    row_of = lambda x, j: jnp.broadcast_to(x[j : j + 1, :], (8, BLOCK))
    column_of = lambda x, l: jnp.broadcast_to(x[:, l : l + 1], (8, BLOCK))
    strips = list(strips)
    for k in range(len(strips)):
        own = strips[k]
        cols = [column_of(own, 8 * k + j) for j in range(8)]
        pivots = (lane >= 8 * k) & (lane < 8 * k + 8)
        s = jnp.where(pivots, jnp.where(lane - 8 * k == sub, 1.0, 0.0), own)
        for j in range(8):
            here = sub == j
            inverse = 1.0 / row_of(cols[j], j)
            factor = jnp.where(here, -1.0, cols[j])
            for q in range(j + 1, 8):
                t = factor * row_of(cols[q], j)
                cols[q] = jnp.where(here, 0.0, cols[q]) - t * inverse
            s = jnp.where(here, 0.0, s) - (factor * row_of(s, j)) * inverse
        rows = [row_of(s, j) for j in range(8)]
        for i in range(len(strips)):
            if i == k:
                continue
            x = strips[i]
            t = [column_of(x, 8 * k + j) * rows[j] for j in range(8)]
            while len(t) > 1:
                t = [t[a] + t[a + 1] for a in range(0, len(t), 2)]
            strips[i] = jnp.where(pivots, 0.0, x) - t[0]
        strips[k] = s
    return jnp.concatenate(strips, axis=0)


def eliminate(a, panel, k):
    at = pl.ds(k * BLOCK, BLOCK)
    inverse = block_inverse([a[pl.ds(k * BLOCK + 8 * i, 8), at] for i in range(BLOCK // 8)])
    panel[...] = exact_matmul(inverse, a[at, :])
    panel[:, at] = inverse
    a[at, at] = jnp.zeros((BLOCK, BLOCK), jnp.float32)
    column = a[:, at]
    a[:, at] = jnp.zeros((POINTS, BLOCK), jnp.float32)
    a[...] = a[...] - exact_matmul(column, panel[...])
    a[at, :] = panel[...]


class Exchange:
    def __init__(self, own, gathered, send_sem, recv_sem, near):
        self.own, self.gathered, self.near = own, gathered, near
        self.send_sem, self.recv_sem = send_sem, recv_sem
        self.copies = {}

    def slot(self, kind, x, half):
        z = self.near["z"] if kind < 2 else 1 - self.near["z"]
        row = (kind % 2) * POINTS + (z * 4 + x) * ROWS + half * HALF
        return self.gathered.at[pl.ds(row, HALF), :]

    def source(self, kind, half):
        if kind == 0:
            return self.own(half)
        return self.slot(kind, self.near["x"], half)

    def send(self, index, src, dst, to):
        copy = pltpu.make_async_remote_copy(
            src_ref=src, dst_ref=dst, send_sem=self.send_sem.at[index], recv_sem=self.recv_sem.at[index],
            device_id=self.near[to], device_id_type=MESH,
        )
        copy.start()
        self.copies[index] = copy

    def arrived(self, index):
        self.copies[index].wait_recv()

    def along_x(self, kind, half):
        dst = self.slot(kind, self.near["x"], half)
        src = self.source(kind, half)
        self.send(XR + 2 * kind + half, src, dst, "right")
        self.send(XL + 2 * kind + half, src, dst, "left")

    def relay_x(self, kind):
        x = self.near["x"]
        self.arrived(XR + 2 * kind)
        block = self.slot(kind, (x + 3) % 4, 0)
        self.send(RR + kind, block, block, "right")
        self.arrived(XL + 2 * kind + 1)
        block = self.slot(kind, (x + 1) % 4, 1)
        self.send(RL + kind, block, block, "left")

    def first(self):
        for half in (0, 1):
            self.send(Y + half, self.own(half), self.slot(1, self.near["x"], half), "across_y")
            self.send(Z + 1 - half, self.own(1 - half), self.slot(0, self.near["x"], 1 - half), "across_z")
        self.along_x(0, 0)
        self.along_x(0, 1)

    def second(self):
        x = self.near["x"]
        self.arrived(Y)
        block = self.slot(1, x, 0)
        self.send(ZC, block, block, "across_z")
        self.along_x(1, 0)
        self.arrived(Z + 1)
        self.send(YC, self.slot(2, x, 1), self.slot(3, x, 1), "across_y")
        self.along_x(2, 1)
        self.relay_x(0)
        self.arrived(Y + 1)
        self.along_x(1, 1)
        self.arrived(Z)
        self.along_x(2, 0)

    def third(self):
        self.arrived(ZC)
        self.along_x(3, 0)
        self.arrived(YC)
        self.along_x(3, 1)
        self.relay_x(1)
        self.relay_x(2)

    def fourth(self):
        self.relay_x(3)

    def last(self):
        for kind in range(4):
            self.arrived(XR + 2 * kind + 1)
            self.arrived(XL + 2 * kind)
            self.arrived(RR + kind)
            self.arrived(RL + kind)

    def sent(self):
        for copy in self.copies.values():
            copy.wait_send()


def kernel(t_ref, ext_ref, map_ref, own_ref, cross_ref, sol_ref,
           iface, outer, other_map, a, panel, send_sem, recv_sem, map_sem):
    sib, leaf = lax.axis_index("sib"), lax.axis_index("leaf")
    leaves = lax.axis_size("leaf")
    x, z = sib % 4, sib // 4
    near = {
        "x": x, "z": z,
        "right": {"sib": z * 4 + (x + 1) % 4},
        "left": {"sib": z * 4 + (x + 3) % 4},
        "across_z": {"sib": (sib + 4) % 8},
        "across_y": {"leaf": (leaf + leaves // 2) % leaves},
    }
    barrier = pltpu.get_barrier_semaphore()
    for name in ("right", "left", "across_z", "across_y"):
        pl.semaphore_signal(barrier, inc=1, device_id=near[name], device_id_type=MESH)
    pl.semaphore_wait(barrier, 4)

    map_copy = pltpu.make_async_remote_copy(
        src_ref=map_ref, dst_ref=other_map, send_sem=map_sem.at[0], recv_sem=map_sem.at[1],
        device_id=near["across_y"], device_id_type=MESH,
    )
    map_copy.start()
    own_half = lambda column: lambda half: t_ref.at[pl.ds(half * HALF, HALF), pl.ds(column, POINTS)]
    g = Exchange(own_half(POINTS), iface, send_sem.at[0], recv_sem.at[0], near)
    r = Exchange(own_half(0), outer, send_sem.at[1], recv_sem.at[1], near)
    g.first()
    mine = pl.ds(pl.multiple_of(sib * ROWS, ROWS), ROWS)
    iface[mine, :] = t_ref[:, POINTS:]
    outer[mine, :] = t_ref[:, :POINTS]
    g.second()
    map_copy.wait()
    point = lax.broadcasted_iota(jnp.int32, (POINTS, POINTS), 0)
    own_onehot = jnp.where(point == map_ref[...], 1.0, 0.0).astype(jnp.bfloat16)
    other_onehot = jnp.where(point == other_map[...], 1.0, 0.0).astype(jnp.bfloat16)
    shuffle = matmul(own_onehot, other_onehot, ((0,), (0,))).astype(jnp.bfloat16)
    g.third()
    g.fourth()
    r.first()
    g.last()
    permuted = select_columns(iface[pl.ds(POINTS, POINTS), :], shuffle, ((1,), (1,)))
    a[...] = iface[pl.ds(0, POINTS), :] + select_rows(shuffle, permuted)
    for k, step in enumerate((r.second, r.third, r.fourth, r.last)):
        eliminate(a, panel, k)
        step()

    wide = outer[pl.ds(0, POINTS), pl.ds(pl.multiple_of(sib // 2 * BLOCK, BLOCK), BLOCK)]
    wide = pltpu.roll(wide, (sib % 2) * ROWS, 1)[:, :ROWS]
    right = product(wide.T, a[...])
    rows = lax.broadcasted_iota(jnp.int32, (ROWS, POINTS), 0) + sib * ROWS
    chosen = select_rows(jnp.where(rows == map_ref[...], 1.0, 0.0).astype(jnp.bfloat16), a[...])
    both = product(jnp.concatenate([right, chosen], axis=0), outer[pl.ds(0, POINTS), :])
    own_ref[...] = ext_ref[...] - both[:ROWS]
    sol_ref[...] = -both[ROWS:]
    moved = select_columns(right, shuffle, ((1,), (0,)))
    cross_ref[...] = -product(moved, outer[pl.ds(POINTS, POINTS), :])
    g.sent()
    r.sent()


def on_device(t_int, t_ext, iface_map):
    vmem = pl.BlockSpec(memory_space=pltpu.VMEM)
    block = jax.ShapeDtypeStruct((ROWS, POINTS), jnp.float32)
    outs = pl.pallas_call(
        kernel,
        out_shape=(block,) * 3,
        in_specs=[vmem] * 3,
        out_specs=(vmem,) * 3,
        scratch_shapes=[
            pltpu.VMEM((2 * POINTS, POINTS), jnp.float32),
            pltpu.VMEM((2 * POINTS, POINTS), jnp.float32),
            pltpu.VMEM((1, POINTS), jnp.int32),
            pltpu.VMEM((POINTS, POINTS), jnp.float32),
            pltpu.VMEM((BLOCK, POINTS), jnp.float32),
            pltpu.SemaphoreType.DMA((2, COPIES)),
            pltpu.SemaphoreType.DMA((2, COPIES)),
            pltpu.SemaphoreType.DMA((2,)),
        ],
        compiler_params=pltpu.CompilerParams(collective_id=0, has_side_effects=True),
    )(t_int[0], t_ext[0], iface_map)
    return tuple(out[None] for out in outs)


def solution(mesh):
    placed = (P("leaf", "sib", None), P("leaf", "sib", None), P("leaf", None))
    return jax.shard_map(
        on_device,
        mesh=mesh,
        in_specs=placed,
        out_specs=(P("leaf", "sib", None),) * 3,
        check_vma=False,
    )
```

time: 359 us -> 77.1 us (0.21); the launches traced: 352 us -> 76.9 us
  other arithmetic: 126 us -> 0 us
  waiting for transfers between devices: 122 us -> 0 us
  Pallas kernels: 0 us -> 73.1 us
  local copies, waits for them, and re-layouts: 56.5 us -> 3.21 us
  matrix products: 21.5 us -> 0 us
  between operations: 17.5 us -> 0.65 us
  starting transfers between devices: 8.66 us -> 0 us
    another operation x20 -> x0, other arithmetic: 121 us -> none  [the longest x15 79.4 us: on_device(): factor = jnp.linalg.cholesky(own_iface + other_iface)]
    all_gather x1 -> x0, waiting for transfers between devices: 102 us -> none  [side_by_side(): lax.all_gather(both, axis, axis=dim, tiled=True)]
    pallas_call x0 -> x1, Pallas kernels: none -> 73.1 us  [on_device(): pl.pallas_call(kernel, out_shape=(block,) * 3, in_specs=[vmem] * 3, out_s...]
    gather x10 -> x0, local copies, waits for them, and re-layouts: 32 us -> none  [the longest x6 22.7 us: common_order(): picked = matrix[inverse]]
    ppermute x2 -> x0, waiting for transfers between devices: 20 us -> none  [partner_2(): lax.ppermute(shard, axis, [(i, i ^ 1 << distance) for i in range(lax.axis...]
    another operation x27 -> x0, matrix products: 18.6 us -> none  [the longest x21 13.1 us: lower_solve(): lax.linalg.triangular_solve(factor, right_side, left_side=True, lower=Tru...]
    another operation x17 -> x0, local copies, waits for them, and re-layouts: 14.1 us -> none  [the longest x13 14 us: lower_solve(): lax.linalg.triangular_solve(factor, right_side, left_side=True, lower=Tru...]
    ppermute x2 -> x0, starting transfers between devices: 8.62 us -> none  [partner_2(): lax.ppermute(shard, axis, [(i, i ^ 1 << distance) for i in range(lax.axis...]
  transfers between devices with their start and end apart: 3 -> 0, of which waited for: 3 -> 0; matrix products, arithmetic and copies ran while one was open for 2% -> 0% of each run, Pallas kernels for 0% -> 0%
where the time goes in v1:
time: 77.1 us; the launch traced here: 76.9 us
  Pallas kernels  73.1 us (95%)
  local copies, waits for them, and re-layouts  3.21 us (4%)
    pallas_call x1, Pallas kernels, on_device(): pl.pallas_call(kernel, out_shape=(block,) * 3, in_specs=[vmem] * 3, out_s...  73.1 us
    unnamed x7, local copies, waits for them, and re-layouts  3.21 us

profile of v1, /device:TPU:56, one launch (start us, length us, event | category | flops | bytes accessed | tf_op | source)
XLA Modules:
  0.0 76.9 jit_solution(17017373808932931080)
XLA Ops:
  0.6 73.1 %shard_map.58 = (f32[64,512]{1,0:T(8,128)}, f32[64,512]{1,0:T(8,128)}, f32[64,512]{1,0:T(8,128)}) custom-call(f32[64,1024]{1,0:T(8,128)} %bitcast.5, f32[64,512]{1,0:T(8,128)} %bitcast.6, s32[1,512]{1,0:T(1,128)} %map_ref.1), custom_call_target="tpu_custom_call" | custom-call | tf_op jit(solution)/shard_map/pallas_call | solution.py:247
  73.7 0.0 copy-start.1
  73.7 1.6 %copy.9 = f32[1,64,512]{2,1,0:T(8,128)} copy(f32[1,64,512]{2,1,0:T(8,128)} %bitcast.9) | data formatting | bytes 262144
  75.3 0.0 copy-done.1
  75.3 0.0 copy-start
  75.3 0.7 copy.10
  76.0 0.3 copy-done
  76.3 0.7 copy.11
Async XLA Ops:
  73.7 1.6 %copy-start.1 = (f32[64,512]{1,0:T(8,128)S(1)}, f32[64,512]{1,0:T(8,128)}, u32[]{:S(2)}) copy-start(f32[64,512]{1,0:T(8,128)} %get-tuple-element.7) | copy-start | bytes 393220
  75.3 1.0 %copy-start = (f32[64,512]{1,0:T(8,128)S(1)}, f32[64,512]{1,0:T(8,128)}, u32[]{:S(2)}) copy-start(f32[64,512]{1,0:T(8,128)} %get-tuple-element.8) | copy-start | bytes 393220

commit v2 on v1

v2 whole, which is shorter than its diff:
```python
import jax
import jax.numpy as jnp
from jax import lax
from jax.experimental import pallas as pl
from jax.experimental.pallas import tpu as pltpu
from jax.sharding import PartitionSpec as P

MESH = pl.DeviceIdType.MESH
POINTS = 512
ROWS = 64
HALF = 32
BLOCK = 128
PANEL = 2
STRIPS = BLOCK // 8
XR, XL, RR, RL, Y, Z, YC, ZC = 0, 16, 32, 48, 64, 68, 72, 76
COPIES = 80


def matmul(a, b, dims=((1,), (0,))):
    return lax.dot_general(a, b, (dims, ((), ())), preferred_element_type=jnp.float32)


def exact_matmul(a, b):
    return jnp.dot(a, b, precision=lax.Precision.HIGHEST, preferred_element_type=jnp.float32)


def thirds(x):
    high = x.astype(jnp.bfloat16)
    rest = x - high.astype(jnp.float32)
    mid = rest.astype(jnp.bfloat16)
    low = (rest - mid.astype(jnp.float32)).astype(jnp.bfloat16)
    return high, mid, low


def halves(x):
    high = x.astype(jnp.bfloat16)
    return high, (x - high.astype(jnp.float32)).astype(jnp.bfloat16)


def select_rows(onehot, x):
    high, mid, low = thirds(x)
    return matmul(onehot, high) + (matmul(onehot, mid) + matmul(onehot, low))


def select_columns(x, onehot, dims):
    high, mid, low = thirds(x)
    return matmul(high, onehot, dims) + (matmul(mid, onehot, dims) + matmul(low, onehot, dims))


def product(a, b):
    a_high, a_low = halves(a)
    b_high, b_low = halves(b)
    return matmul(a_high, b_high) + (matmul(a_high, b_low) + matmul(a_low, b_high))


def pivot_panel(own, first):
    lane = lax.broadcasted_iota(jnp.int32, (8, BLOCK), 1)
    sub = lax.broadcasted_iota(jnp.int32, (8, BLOCK), 0)
    width = 8 * len(own)
    cols = [[column_of(x, 8 * first + j) for x in own] for j in range(width)]
    pivots = (lane >= 8 * first) & (lane < 8 * first + width)
    s = [jnp.where(pivots, jnp.where(lane - 8 * (first + n) == sub, 1.0, 0.0), x) for n, x in enumerate(own)]
    for j in range(width):
        at, row = divmod(j, 8)
        here = sub == row
        inverse = 1.0 / row_of(cols[j][at], row)
        factor = [jnp.where(here, -1.0, x) if n == at else x for n, x in enumerate(cols[j])]

        def reduced(xs):
            r = row_of(xs[at], row)
            return [(jnp.where(here, 0.0, x) if n == at else x) - (f * r) * inverse for n, (x, f) in enumerate(zip(xs, factor))]

        for q in range(j + 1, width):
            cols[q] = reduced(cols[q])
        s = reduced(s)
    return s, pivots


def row_of(x, j):
    return jnp.broadcast_to(x[j : j + 1, :], (8, BLOCK))


def column_of(x, lane):
    return jnp.broadcast_to(x[:, lane : lane + 1], (8, BLOCK))


def block_inverse(strips):
    strips = list(strips)
    for k in range(0, STRIPS, PANEL):
        s, pivots = pivot_panel(strips[k : k + PANEL], k)
        soon = range(k + PANEL, min(STRIPS, k + 2 * PANEL))
        rest = [i for i in range(STRIPS) if not k <= i < k + PANEL and i not in soon]
        old = list(strips)
        for i in soon:
            t = [column_of(old[i], 8 * k + j) * row_of(s[j // 8], j % 8) for j in range(8 * PANEL)]
            while len(t) > 1:
                t = [t[n] + t[n + 1] for n in range(0, len(t), 2)]
            strips[i] = jnp.where(pivots, 0.0, old[i]) - t[0]
        left = jnp.concatenate([jnp.where(pivots, old[i], 0.0) for i in rest], axis=0)
        zero = jnp.zeros((8, BLOCK), jnp.float32)
        right = jnp.concatenate([s[i - k] if k <= i < k + PANEL else zero for i in range(STRIPS)], axis=0)
        change = exact_matmul(left, right)
        for n, i in enumerate(rest):
            strips[i] = jnp.where(pivots, 0.0, old[i]) - change[8 * n : 8 * n + 8]
        strips[k : k + PANEL] = s
    return jnp.concatenate(strips, axis=0)


def eliminate(a, panel, k):
    at = pl.ds(k * BLOCK, BLOCK)
    inverse = block_inverse([a[pl.ds(k * BLOCK + 8 * i, 8), at] for i in range(BLOCK // 8)])
    panel[...] = exact_matmul(inverse, a[at, :])
    panel[:, at] = inverse
    a[at, at] = jnp.zeros((BLOCK, BLOCK), jnp.float32)
    column = a[:, at]
    a[:, at] = jnp.zeros((POINTS, BLOCK), jnp.float32)
    a[...] = a[...] - exact_matmul(column, panel[...])
    a[at, :] = panel[...]


class Exchange:
    def __init__(self, own, view, send_sem, recv_sem, near, has_more):
        self.own, self.view, self.near, self.has_more = own, view, near, has_more
        self.send_sem, self.recv_sem = send_sem, recv_sem

    def copy(self, index, src, dst, to):
        return pltpu.make_async_remote_copy(
            src_ref=src, dst_ref=dst, send_sem=self.send_sem.at[index], recv_sem=self.recv_sem.at[index],
            device_id=self.near[to], device_id_type=MESH,
        )

    def over_y(self, c):
        return self.copy(Y + c, self.own(c), self.view(1, self.near["x"], c), "across_y")

    def over_z(self, c):
        return self.copy(Z + c, self.own(c), self.view(0, self.near["x"], c), "across_z")

    def corner(self, c):
        x = self.near["x"]
        if c % 2:
            return self.copy(YC + c, self.view(2, x, c), self.view(3, x, c), "across_y")
        return self.copy(ZC + c, self.view(1, x, c), self.view(1, x, c), "across_z")

    def to_right(self, kind, c):
        x = self.near["x"]
        src = self.own(c) if kind == 0 else self.view(kind, x, c)
        return self.copy(XR + 4 * kind + c, src, self.view(kind, x, c), "right")

    def to_left(self, kind, c):
        x = self.near["x"]
        src = self.own(c) if kind == 0 else self.view(kind, x, c)
        return self.copy(XL + 4 * kind + c, src, self.view(kind, x, c), "left")

    def onward(self, kind, c):
        x = self.near["x"]
        if c % 2:
            block = self.view(kind, (x + 1) % 4, c)
            return self.copy(RL + 4 * kind + c, block, block, "left")
        block = self.view(kind, (x + 3) % 4, c)
        return self.copy(RR + 4 * kind + c, block, block, "right")

    def along_x(self, kind, c):
        self.to_right(kind, c).start()
        self.to_left(kind, c).start()

    def relay_x(self, kind, c):
        (self.to_left if c % 2 else self.to_right)(kind, c).wait_recv()
        self.onward(kind, c).start()

    def more(self, kind, run):
        if self.has_more is not None:
            pl.when(self.has_more(kind))(run)

    def first(self):
        def run(even, odd):
            self.over_y(even).start()
            self.over_z(odd).start()
            self.along_x(0, even)
            self.along_x(0, odd)
            self.over_y(odd).start()
            self.over_z(even).start()

        run(0, 1)
        self.more(0, lambda: run(2, 3))

    def second(self):
        def from_y(even, odd):
            self.over_y(even).wait_recv()
            self.corner(even).start()
            self.along_x(1, even)

        def from_z(even, odd):
            self.over_z(odd).wait_recv()
            self.corner(odd).start()
            self.along_x(2, odd)

        def own(even, odd):
            self.relay_x(0, even)
            self.relay_x(0, odd)

        def late_y(even, odd):
            self.over_y(odd).wait_recv()
            self.along_x(1, odd)

        def late_z(even, odd):
            self.over_z(even).wait_recv()
            self.along_x(2, even)

        for step in (from_y, from_z, own, late_y, late_z):
            step(0, 1)

        def more_here():
            own(2, 3)
            from_y(2, 3)
            late_y(2, 3)

        def more_there():
            from_z(2, 3)
            late_z(2, 3)

        self.more(0, more_here)
        self.more(2, more_there)

    def third(self):
        def corners(even, odd):
            self.corner(even).wait_recv()
            self.along_x(3, even)
            self.corner(odd).wait_recv()
            self.along_x(3, odd)

        def relay(kind, even, odd):
            self.relay_x(kind, even)
            self.relay_x(kind, odd)

        corners(0, 1)
        relay(1, 0, 1)
        relay(2, 0, 1)
        self.more(0, lambda: relay(1, 2, 3))

        def more_there():
            corners(2, 3)
            relay(2, 2, 3)

        self.more(2, more_there)

    def fourth(self):
        def relay(even, odd):
            self.relay_x(3, even)
            self.relay_x(3, odd)

        relay(0, 1)
        self.more(3, lambda: relay(2, 3))

    def last(self, kind):
        def run(even, odd):
            self.to_right(kind, odd).wait_recv()
            self.to_left(kind, even).wait_recv()
            self.onward(kind, even).wait_recv()
            self.onward(kind, odd).wait_recv()

        run(0, 1)
        self.more(kind, lambda: run(2, 3))

    def sent(self):
        def along(kind, even, odd):
            for c in (even, odd):
                self.to_right(kind, c).wait_send()
                self.to_left(kind, c).wait_send()
                self.onward(kind, c).wait_send()

        def across(even, odd):
            for c in (even, odd):
                self.over_y(c).wait_send()
                self.over_z(c).wait_send()

        across(0, 1)
        self.corner(0).wait_send()
        self.corner(1).wait_send()
        for kind in range(4):
            along(kind, 0, 1)

        def more_here():
            across(2, 3)
            self.corner(2).wait_send()
            along(0, 2, 3)
            along(1, 2, 3)

        def more_there():
            self.corner(3).wait_send()
            along(2, 2, 3)
            along(3, 2, 3)

        self.more(0, more_here)
        self.more(2, more_there)


def place_rows(tiles, matrix, box, half):
    rows = pl.ds(pl.multiple_of(half * 4 * ROWS, 4 * ROWS), 4 * ROWS)
    matrix[rows, :] = jnp.zeros((4 * ROWS, POINTS), jnp.float32)
    for x in range(4):
        block = box * 8 + half * 4 + x
        tile = 2 * half + x // 2
        at = pl.ds(pl.multiple_of((half * 4 + x) * ROWS, ROWS), ROWS)
        for t in range(3):
            lanes = pl.ds(pl.multiple_of((tile + t) % 4 * BLOCK, BLOCK), BLOCK)
            matrix[at, lanes] = tiles[block, t] * (0.5 if t == 0 else 1.0)
    return rows


def kernel(t_ref, map_ref, raw_ref, tiles, outer, other_map, near_part, far_part, shuffle, a, panel, send_sem, recv_sem, map_sem):
    sib, leaf = lax.axis_index("sib"), lax.axis_index("leaf")
    leaves = lax.axis_size("leaf")
    x, z = sib % 4, sib // 4
    near = {
        "x": x, "z": z,
        "right": {"sib": z * 4 + (x + 1) % 4},
        "left": {"sib": z * 4 + (x + 3) % 4},
        "across_z": {"sib": (sib + 4) % 8},
        "across_y": {"leaf": (leaf + leaves // 2) % leaves},
    }
    barrier = pltpu.get_barrier_semaphore()
    for name in ("right", "left", "across_z", "across_y"):
        pl.semaphore_signal(barrier, inc=1, device_id=near[name], device_id_type=MESH)
    pl.semaphore_wait(barrier, 4)

    map_copy = pltpu.make_async_remote_copy(
        src_ref=map_ref, dst_ref=other_map, send_sem=map_sem.at[0], recv_sem=map_sem.at[1],
        device_id=near["across_y"], device_id_type=MESH,
    )
    map_copy.start()

    def z_of(kind):
        return z if kind < 2 else 1 - z

    def own_tile(c):
        lanes = pl.ds(pl.multiple_of(POINTS + (sib // 2 + min(c, 2)) % 4 * BLOCK, BLOCK), BLOCK)
        return t_ref.at[:, lanes] if c < 2 else t_ref.at[pl.ds((c - 2) * HALF, HALF), lanes]

    def tile_view(kind, x, c):
        block = tiles.at[kind % 2 * 8 + z_of(kind) * 4 + x, min(c, 2)]
        return block if c < 2 else block.at[pl.ds((c - 2) * HALF, HALF), :]

    def own_rows(c):
        return t_ref.at[pl.ds(c * HALF, HALF), pl.ds(0, POINTS)]

    def row_view(kind, x, c):
        return outer.at[pl.ds(kind % 2 * POINTS + (z_of(kind) * 4 + x) * ROWS + c * HALF, HALF), :]

    g = Exchange(own_tile, tile_view, send_sem.at[0], recv_sem.at[0], near, lambda kind: z_of(kind) == 0)
    r = Exchange(own_rows, row_view, send_sem.at[1], recv_sem.at[1], near, None)
    g.first()
    mine = pl.ds(pl.multiple_of(sib * ROWS, ROWS), ROWS)
    outer[mine, :] = t_ref[:, :POINTS]
    for t in range(2):
        tiles[sib, t] = t_ref[:, pl.ds(pl.multiple_of(POINTS + (sib // 2 + t) % 4 * BLOCK, BLOCK), BLOCK)]

    @pl.when(z == 0)
    def _():
        tiles[sib, 2] = t_ref[:, pl.ds(pl.multiple_of(POINTS + (sib // 2 + 2) % 4 * BLOCK, BLOCK), BLOCK)]

    for block in (4, 5, 6, 7, 12, 13, 14, 15):
        tiles[block, 2] = jnp.zeros((ROWS, BLOCK), jnp.float32)
    g.second()
    map_copy.wait()
    point = lax.broadcasted_iota(jnp.int32, (POINTS, POINTS), 0)
    own_onehot = jnp.where(point == map_ref[...], 1.0, 0.0).astype(jnp.bfloat16)
    other_onehot = jnp.where(point == other_map[...], 1.0, 0.0).astype(jnp.bfloat16)
    shuffle[...] = matmul(own_onehot, other_onehot, ((0,), (0,))).astype(jnp.bfloat16)
    g.third()
    g.fourth()
    r.first()

    def permuted(half):
        rows = place_rows(tiles, far_part, 1, half)
        moved = select_columns(far_part[rows, :], shuffle[...], ((1,), (1,)))
        lanes = pl.ds(pl.multiple_of(half * 4 * ROWS, 4 * ROWS), 4 * ROWS)
        return select_rows(shuffle[:, lanes], moved)

    g.last(1)
    near_part[...] = permuted(z)
    g.last(0)
    place_rows(tiles, a, 0, z)
    g.last(2)
    place_rows(tiles, a, 0, 1 - z)
    g.last(3)
    near_part[...] = (near_part[...] + a[...]) + permuted(1 - z)
    for i in range(4):
        for j in range(4):
            rows, lanes = pl.ds(i * BLOCK, BLOCK), pl.ds(j * BLOCK, BLOCK)
            a[rows, lanes] = near_part[rows, lanes] + near_part[lanes, rows].T

    def finish():
        for kind in range(4):
            r.last(kind)

    for k, step in enumerate((r.second, r.third, r.fourth, finish)):
        eliminate(a, panel, k)
        step()

    wide = outer[pl.ds(0, POINTS), pl.ds(pl.multiple_of(sib // 2 * BLOCK, BLOCK), BLOCK)]
    wide = pltpu.roll(wide, (sib % 2) * ROWS, 1)[:, :ROWS]
    right = product(wide.T, a[...])
    rows = lax.broadcasted_iota(jnp.int32, (ROWS, POINTS), 0) + sib * ROWS
    chosen = select_rows(jnp.where(rows == map_ref[...], 1.0, 0.0).astype(jnp.bfloat16), a[...])
    raw_ref[: 2 * ROWS] = product(jnp.concatenate([right, chosen], axis=0), outer[pl.ds(0, POINTS), :])
    moved = select_columns(right, shuffle[...], ((1,), (0,)))
    raw_ref[2 * ROWS :] = product(moved, outer[pl.ds(POINTS, POINTS), :])
    g.sent()
    r.sent()


def outputs(raw_ref, ext_ref, own_ref, cross_ref, sol_ref):
    own_ref[...] = ext_ref[...] - raw_ref[:ROWS]
    sol_ref[...] = -raw_ref[ROWS : 2 * ROWS]
    cross_ref[...] = -raw_ref[2 * ROWS :]


def on_device(t_int, t_ext, iface_map):
    vmem = pl.BlockSpec(memory_space=pltpu.VMEM)
    raw = pl.pallas_call(
        kernel,
        out_shape=jax.ShapeDtypeStruct((3 * ROWS, POINTS), jnp.float32),
        in_specs=[vmem] * 2,
        out_specs=vmem,
        scratch_shapes=[
            pltpu.VMEM((16, 3, ROWS, BLOCK), jnp.float32),
            pltpu.VMEM((2 * POINTS, POINTS), jnp.float32),
            pltpu.VMEM((1, POINTS), jnp.int32),
            pltpu.VMEM((POINTS, POINTS), jnp.float32),
            pltpu.VMEM((POINTS, POINTS), jnp.float32),
            pltpu.VMEM((POINTS, POINTS), jnp.bfloat16),
            pltpu.VMEM((POINTS, POINTS), jnp.float32),
            pltpu.VMEM((BLOCK, POINTS), jnp.float32),
            pltpu.SemaphoreType.DMA((2, COPIES)),
            pltpu.SemaphoreType.DMA((2, COPIES)),
            pltpu.SemaphoreType.DMA((2,)),
        ],
        compiler_params=pltpu.CompilerParams(collective_id=0, has_side_effects=True),
    )(t_int[0], iface_map)
    block = jax.ShapeDtypeStruct((ROWS, POINTS), jnp.float32)
    outs = pl.pallas_call(outputs, out_shape=(block,) * 3, in_specs=[vmem] * 2, out_specs=(vmem,) * 3)(raw, t_ext[0])
    return tuple(out[None] for out in outs)


def solution(mesh):
    placed = (P("leaf", "sib", None), P("leaf", "sib", None), P("leaf", None))
    return jax.shard_map(
        on_device,
        mesh=mesh,
        in_specs=placed,
        out_specs=(P("leaf", "sib", None),) * 3,
        check_vma=False,
    )
```

time: 77.1 us -> 62.7 us (0.81)
  Pallas kernels: 73.1 us -> 61.6 us
  local copies, waits for them, and re-layouts: 3.21 us -> 0 us
    pallas_call x1 -> x2, Pallas kernels: 73.1 us -> 61.6 us  [the longest x1 59.8 us: on_device(): pl.pallas_call(kernel, out_shape=jax.ShapeDtypeStruct((3 * ROWS, POINTS),...]
    unnamed x7 -> x0, local copies, waits for them, and re-layouts: 3.21 us -> none
where the time goes in v2:
time: 62.7 us; the launch traced here: 62.2 us
  Pallas kernels  61.6 us (98%)
  between operations  0.64 us (1%)
    pallas_call x1, Pallas kernels, on_device(): pl.pallas_call(kernel, out_shape=jax.ShapeDtypeStruct((3 * ROWS, POINTS),...  59.8 us
    pallas_call x1, Pallas kernels, on_device(): pl.pallas_call(outputs, out_shape=(block,) * 3, in_specs=[vmem] * 2, out_...  1.78 us

profile of v2, /device:TPU:56, one launch (start us, length us, event | category | flops | bytes accessed | tf_op | source)
XLA Modules:
  0.0 62.2 jit_solution(15775612843322706021)
XLA Ops:
  0.6 59.8 %shard_map.58.raw_ref = f32[192,512]{1,0:T(8,128)} custom-call(f32[64,1024]{1,0:T(8,128)} %bitcast.5, s32[1,512]{1,0:T(1,128)} %map_ref.1), custom_call_target="tpu_custom_call" | custom-call | tf_op jit(solution)/shard_map/pallas_call | solution.py:420
  60.4 1.8 %shard_map.59 = (f32[64,512]{1,0:T(8,128)}, f32[64,512]{1,0:T(8,128)}, f32[64,512]{1,0:T(8,128)}) custom-call(f32[192,512]{1,0:T(8,128)} %shard_map.58.raw_ref, f32[64,512]{1,0:T(8,128)} %bitcast.6), custom_call_target="tpu_custom_call" | custom-call | tf_op jit(solution)/shard_map/pallas_call | solution.py:441

commit v3 on v2

--- a/solution.py
+++ b/solution.py
@@ -12,8 +12,8 @@
 BLOCK = 128
 PANEL = 2
 STRIPS = BLOCK // 8
-XR, XL, RR, RL, Y, Z, YC, ZC = 0, 16, 32, 48, 64, 68, 72, 76
-COPIES = 80
+XR, XL, XO, Y, Z, YC, ZC = 0, 16, 32, 48, 52, 56, 60
+COPIES = 64
 
 
 def matmul(a, b, dims=((1,), (0,))):
@@ -106,16 +106,23 @@
     return jnp.concatenate(strips, axis=0)
 
 
-def eliminate(a, panel, k):
-    at = pl.ds(k * BLOCK, BLOCK)
-    inverse = block_inverse([a[pl.ds(k * BLOCK + 8 * i, 8), at] for i in range(BLOCK // 8)])
-    panel[...] = exact_matmul(inverse, a[at, :])
-    panel[:, at] = inverse
-    a[at, at] = jnp.zeros((BLOCK, BLOCK), jnp.float32)
-    column = a[:, at]
-    a[:, at] = jnp.zeros((POINTS, BLOCK), jnp.float32)
-    a[...] = a[...] - exact_matmul(column, panel[...])
-    a[at, :] = panel[...]
+def invert(a, panel, between):
+    diagonal = [a[pl.ds(8 * i, 8), pl.ds(0, BLOCK)] for i in range(STRIPS)]
+    for k in range(POINTS // BLOCK):
+        at, after = pl.ds(k * BLOCK, BLOCK), pl.ds((k + 1) * BLOCK, BLOCK)
+        inverse = block_inverse(diagonal)
+        between[2 * k]()
+        if (k + 1) * BLOCK < POINTS:
+            ahead = a[after, after] - exact_matmul(a[after, at], exact_matmul(inverse, a[at, after]))
+            diagonal = [ahead[8 * i : 8 * i + 8] for i in range(STRIPS)]
+        panel[...] = exact_matmul(inverse, a[at, :])
+        panel[:, at] = inverse
+        a[at, at] = jnp.zeros((BLOCK, BLOCK), jnp.float32)
+        column = a[:, at]
+        a[:, at] = jnp.zeros((POINTS, BLOCK), jnp.float32)
+        a[...] = a[...] - exact_matmul(column, panel[...])
+        a[at, :] = panel[...]
+        between[2 * k + 1]()
 
 
 class Exchange:
@@ -151,21 +158,15 @@
         src = self.own(c) if kind == 0 else self.view(kind, x, c)
         return self.copy(XL + 4 * kind + c, src, self.view(kind, x, c), "left")
 
-    def onward(self, kind, c):
+    def to_opposite(self, kind, c):
         x = self.near["x"]
-        if c % 2:
-            block = self.view(kind, (x + 1) % 4, c)
-            return self.copy(RL + 4 * kind + c, block, block, "left")
-        block = self.view(kind, (x + 3) % 4, c)
-        return self.copy(RR + 4 * kind + c, block, block, "right")
+        src = self.own(c) if kind == 0 else self.view(kind, x, c)
+        return self.copy(XO + 4 * kind + c, src, self.view(kind, x, c), "opposite")
 
     def along_x(self, kind, c):
         self.to_right(kind, c).start()
         self.to_left(kind, c).start()
-
-    def relay_x(self, kind, c):
-        (self.to_left if c % 2 else self.to_right)(kind, c).wait_recv()
-        self.onward(kind, c).start()
+        self.to_opposite(kind, c).start()
 
     def more(self, kind, run):
         if self.has_more is not None:
@@ -194,10 +195,6 @@
             self.corner(odd).start()
             self.along_x(2, odd)
 
-        def own(even, odd):
-            self.relay_x(0, even)
-            self.relay_x(0, odd)
-
         def late_y(even, odd):
             self.over_y(odd).wait_recv()
             self.along_x(1, odd)
@@ -206,11 +203,10 @@
             self.over_z(even).wait_recv()
             self.along_x(2, even)
 
-        for step in (from_y, from_z, own, late_y, late_z):
+        for step in (from_y, from_z, late_y, late_z):
             step(0, 1)
 
         def more_here():
-            own(2, 3)
             from_y(2, 3)
             late_y(2, 3)
 
@@ -228,35 +224,15 @@
             self.corner(odd).wait_recv()
             self.along_x(3, odd)
 
-        def relay(kind, even, odd):
-            self.relay_x(kind, even)
-            self.relay_x(kind, odd)
-
         corners(0, 1)
-        relay(1, 0, 1)
-        relay(2, 0, 1)
-        self.more(0, lambda: relay(1, 2, 3))
-
-        def more_there():
-            corners(2, 3)
-            relay(2, 2, 3)
-
-        self.more(2, more_there)
-
-    def fourth(self):
-        def relay(even, odd):
-            self.relay_x(3, even)
-            self.relay_x(3, odd)
-
-        relay(0, 1)
-        self.more(3, lambda: relay(2, 3))
+        self.more(2, lambda: corners(2, 3))
 
     def last(self, kind):
         def run(even, odd):
-            self.to_right(kind, odd).wait_recv()
-            self.to_left(kind, even).wait_recv()
-            self.onward(kind, even).wait_recv()
-            self.onward(kind, odd).wait_recv()
+            for c in (even, odd):
+                self.to_right(kind, c).wait_recv()
+                self.to_left(kind, c).wait_recv()
+                self.to_opposite(kind, c).wait_recv()
 
         run(0, 1)
         self.more(kind, lambda: run(2, 3))
@@ -266,7 +242,7 @@
             for c in (even, odd):
                 self.to_right(kind, c).wait_send()
                 self.to_left(kind, c).wait_send()
-                self.onward(kind, c).wait_send()
+                self.to_opposite(kind, c).wait_send()
 
         def across(even, odd):
             for c in (even, odd):
@@ -307,7 +283,7 @@
     return rows
 
 
-def kernel(t_ref, map_ref, raw_ref, tiles, outer, other_map, near_part, far_part, shuffle, a, panel, send_sem, recv_sem, map_sem):
+def kernel(t_ref, map_ref, raw_ref, tiles, outer, other_map, near_part, far_part, shuffle, a, panel, send_sem, recv_sem, map_sem, keep_sem):
     sib, leaf = lax.axis_index("sib"), lax.axis_index("leaf")
     leaves = lax.axis_size("leaf")
     x, z = sib % 4, sib // 4
@@ -315,13 +291,14 @@
         "x": x, "z": z,
         "right": {"sib": z * 4 + (x + 1) % 4},
         "left": {"sib": z * 4 + (x + 3) % 4},
+        "opposite": {"sib": z * 4 + (x + 2) % 4},
         "across_z": {"sib": (sib + 4) % 8},
         "across_y": {"leaf": (leaf + leaves // 2) % leaves},
     }
     barrier = pltpu.get_barrier_semaphore()
-    for name in ("right", "left", "across_z", "across_y"):
+    for name in ("right", "left", "opposite", "across_z", "across_y"):
         pl.semaphore_signal(barrier, inc=1, device_id=near[name], device_id_type=MESH)
-    pl.semaphore_wait(barrier, 4)
+    pl.semaphore_wait(barrier, 5)
 
     map_copy = pltpu.make_async_remote_copy(
         src_ref=map_ref, dst_ref=other_map, send_sem=map_sem.at[0], recv_sem=map_sem.at[1],
@@ -349,14 +326,17 @@
     g = Exchange(own_tile, tile_view, send_sem.at[0], recv_sem.at[0], near, lambda kind: z_of(kind) == 0)
     r = Exchange(own_rows, row_view, send_sem.at[1], recv_sem.at[1], near, None)
     g.first()
-    mine = pl.ds(pl.multiple_of(sib * ROWS, ROWS), ROWS)
-    outer[mine, :] = t_ref[:, :POINTS]
-    for t in range(2):
-        tiles[sib, t] = t_ref[:, pl.ds(pl.multiple_of(POINTS + (sib // 2 + t) % 4 * BLOCK, BLOCK), BLOCK)]
-
-    @pl.when(z == 0)
-    def _():
-        tiles[sib, 2] = t_ref[:, pl.ds(pl.multiple_of(POINTS + (sib // 2 + 2) % 4 * BLOCK, BLOCK), BLOCK)]
+
+    def keep(n):
+        if n == 3:
+            mine = pl.ds(pl.multiple_of(sib * ROWS, ROWS), ROWS)
+            return pltpu.make_async_copy(t_ref.at[:, pl.ds(0, POINTS)], outer.at[mine, :], keep_sem.at[n])
+        lanes = pl.ds(pl.multiple_of(POINTS + (sib // 2 + n) % 4 * BLOCK, BLOCK), BLOCK)
+        return pltpu.make_async_copy(t_ref.at[:, lanes], tiles.at[sib, n], keep_sem.at[n])
+
+    for n in (0, 1, 3):
+        keep(n).start()
+    pl.when(z == 0)(lambda: keep(2).start())
 
     for block in (4, 5, 6, 7, 12, 13, 14, 15):
         tiles[block, 2] = jnp.zeros((ROWS, BLOCK), jnp.float32)
@@ -367,8 +347,10 @@
     other_onehot = jnp.where(point == other_map[...], 1.0, 0.0).astype(jnp.bfloat16)
     shuffle[...] = matmul(own_onehot, other_onehot, ((0,), (0,))).astype(jnp.bfloat16)
     g.third()
-    g.fourth()
     r.first()
+    for n in (0, 1, 3):
+        keep(n).wait()
+    pl.when(z == 0)(lambda: keep(2).wait())
 
     def permuted(half):
         rows = place_rows(tiles, far_part, 1, half)
@@ -389,21 +371,22 @@
             rows, lanes = pl.ds(i * BLOCK, BLOCK), pl.ds(j * BLOCK, BLOCK)
             a[rows, lanes] = near_part[rows, lanes] + near_part[lanes, rows].T
 
-    def finish():
-        for kind in range(4):
-            r.last(kind)
-
-    for k, step in enumerate((r.second, r.third, r.fourth, finish)):
-        eliminate(a, panel, k)
-        step()
-
+    def nothing():
+        pass
+
+    invert(a, panel, (r.second, nothing, nothing, r.third, nothing, nothing, nothing, nothing))
+
+    rows = lax.broadcasted_iota(jnp.int32, (ROWS, POINTS), 0) + sib * ROWS
+    chosen = select_rows(jnp.where(rows == map_ref[...], 1.0, 0.0).astype(jnp.bfloat16), a[...])
+    r.last(0)
+    r.last(2)
     wide = outer[pl.ds(0, POINTS), pl.ds(pl.multiple_of(sib // 2 * BLOCK, BLOCK), BLOCK)]
     wide = pltpu.roll(wide, (sib % 2) * ROWS, 1)[:, :ROWS]
     right = product(wide.T, a[...])
-    rows = lax.broadcasted_iota(jnp.int32, (ROWS, POINTS), 0) + sib * ROWS
-    chosen = select_rows(jnp.where(rows == map_ref[...], 1.0, 0.0).astype(jnp.bfloat16), a[...])
     raw_ref[: 2 * ROWS] = product(jnp.concatenate([right, chosen], axis=0), outer[pl.ds(0, POINTS), :])
     moved = select_columns(right, shuffle[...], ((1,), (0,)))
+    r.last(1)
+    r.last(3)
     raw_ref[2 * ROWS :] = product(moved, outer[pl.ds(POINTS, POINTS), :])
     g.sent()
     r.sent()
@@ -420,7 +403,7 @@
     raw = pl.pallas_call(
         kernel,
         out_shape=jax.ShapeDtypeStruct((3 * ROWS, POINTS), jnp.float32),
-        in_specs=[vmem] * 2,
+        in_specs=[pl.BlockSpec(memory_space=pl.ANY), vmem],
         out_specs=vmem,
         scratch_shapes=[
             pltpu.VMEM((16, 3, ROWS, BLOCK), jnp.float32),
@@ -434,6 +417,7 @@
             pltpu.SemaphoreType.DMA((2, COPIES)),
             pltpu.SemaphoreType.DMA((2, COPIES)),
             pltpu.SemaphoreType.DMA((2,)),
+            pltpu.SemaphoreType.DMA((4,)),
         ],
         compiler_params=pltpu.CompilerParams(collective_id=0, has_side_effects=True),
     )(t_int[0], iface_map)

time: 62.7 us -> 59.4 us (0.947)
  Pallas kernels: 61.6 us -> 57.7 us
    pallas_call x1, Pallas kernels: 59.8 us -> 55.9 us  [on_device(): pl.pallas_call(kernel, out_shape=jax.ShapeDtypeStruct((3 * ROWS, POINTS),...]
where the time goes in v3:
time: 59.4 us; the launch traced here: 58.3 us
  Pallas kernels  57.7 us (97%)
  between operations  0.64 us (1%)
    pallas_call x1, Pallas kernels, on_device(): pl.pallas_call(kernel, out_shape=jax.ShapeDtypeStruct((3 * ROWS, POINTS),...  55.9 us
    pallas_call x1, Pallas kernels, on_device(): pl.pallas_call(outputs, out_shape=(block,) * 3, in_specs=[vmem] * 2, out_...  1.78 us

profile of v3, /device:TPU:56, one launch (start us, length us, event | category | flops | bytes accessed | tf_op | source)
XLA Modules:
  0.0 58.3 jit_solution(7479775744422704043)
XLA Ops:
  0.6 55.9 %shard_map.58.raw_ref = f32[192,512]{1,0:T(8,128)} custom-call(f32[64,1024]{1,0:T(8,128)} %bitcast.5, s32[1,512]{1,0:T(1,128)} %map_ref.1), custom_call_target="tpu_custom_call" | custom-call | tf_op jit(solution)/shard_map/pallas_call | solution.py:403
  56.6 1.8 %shard_map.59 = (f32[64,512]{1,0:T(8,128)}, f32[64,512]{1,0:T(8,128)}, f32[64,512]{1,0:T(8,128)}) custom-call(f32[192,512]{1,0:T(8,128)} %shard_map.58.raw_ref, f32[64,512]{1,0:T(8,128)} %bitcast.6), custom_call_target="tpu_custom_call" | custom-call | tf_op jit(solution)/shard_map/pallas_call | solution.py:425

commit v4 on v3

--- a/solution.py
+++ b/solution.py
@@ -126,8 +126,8 @@
 
 
 class Exchange:
-    def __init__(self, own, view, send_sem, recv_sem, near, has_more):
-        self.own, self.view, self.near, self.has_more = own, view, near, has_more
+    def __init__(self, own, view, send_sem, recv_sem, near, has_more, relayed):
+        self.own, self.view, self.near, self.has_more, self.relayed = own, view, near, has_more, relayed
         self.send_sem, self.recv_sem = send_sem, recv_sem
 
     def copy(self, index, src, dst, to):
@@ -160,13 +160,23 @@
 
     def to_opposite(self, kind, c):
         x = self.near["x"]
+        if self.relayed:
+            block = self.view(kind, (x + (1 if c % 2 else 3)) % 4, c)
+            return self.copy(XO + 4 * kind + c, block, block, "left" if c % 2 else "right")
         src = self.own(c) if kind == 0 else self.view(kind, x, c)
         return self.copy(XO + 4 * kind + c, src, self.view(kind, x, c), "opposite")
 
     def along_x(self, kind, c):
         self.to_right(kind, c).start()
         self.to_left(kind, c).start()
-        self.to_opposite(kind, c).start()
+        if not self.relayed:
+            self.to_opposite(kind, c).start()
+
+    def relay(self, kind):
+        self.to_right(kind, 0).wait_recv()
+        self.to_opposite(kind, 0).start()
+        self.to_left(kind, 1).wait_recv()
+        self.to_opposite(kind, 1).start()
 
     def more(self, kind, run):
         if self.has_more is not None:
@@ -230,8 +240,10 @@
     def last(self, kind):
         def run(even, odd):
             for c in (even, odd):
-                self.to_right(kind, c).wait_recv()
-                self.to_left(kind, c).wait_recv()
+                if c % 2 or not self.relayed:
+                    self.to_right(kind, c).wait_recv()
+                if c % 2 == 0 or not self.relayed:
+                    self.to_left(kind, c).wait_recv()
                 self.to_opposite(kind, c).wait_recv()
 
         run(0, 1)
@@ -283,7 +295,7 @@
     return rows
 
 
-def kernel(t_ref, map_ref, raw_ref, tiles, outer, other_map, near_part, far_part, shuffle, a, panel, send_sem, recv_sem, map_sem, keep_sem):
+def kernel(t_ref, map_ref, ext_ref, raw_ref, tiles, outer, other_map, near_part, far_part, shuffle, a, panel, send_sem, recv_sem, map_sem, keep_sem):
     sib, leaf = lax.axis_index("sib"), lax.axis_index("leaf")
     leaves = lax.axis_size("leaf")
     x, z = sib % 4, sib // 4
@@ -323,8 +335,8 @@
     def row_view(kind, x, c):
         return outer.at[pl.ds(kind % 2 * POINTS + (z_of(kind) * 4 + x) * ROWS + c * HALF, HALF), :]
 
-    g = Exchange(own_tile, tile_view, send_sem.at[0], recv_sem.at[0], near, lambda kind: z_of(kind) == 0)
-    r = Exchange(own_rows, row_view, send_sem.at[1], recv_sem.at[1], near, None)
+    g = Exchange(own_tile, tile_view, send_sem.at[0], recv_sem.at[0], near, lambda kind: z_of(kind) == 0, False)
+    r = Exchange(own_rows, row_view, send_sem.at[1], recv_sem.at[1], near, None, True)
     g.first()
 
     def keep(n):
@@ -336,6 +348,8 @@
 
     for n in (0, 1, 3):
         keep(n).start()
+    ext_copy = pltpu.make_async_copy(ext_ref, raw_ref.at[pl.ds(0, ROWS), :], keep_sem.at[4])
+    ext_copy.start()
     pl.when(z == 0)(lambda: keep(2).start())
 
     for block in (4, 5, 6, 7, 12, 13, 14, 15):
@@ -350,6 +364,7 @@
     r.first()
     for n in (0, 1, 3):
         keep(n).wait()
+    ext_copy.wait()
     pl.when(z == 0)(lambda: keep(2).wait())
 
     def permuted(half):
@@ -374,7 +389,20 @@
     def nothing():
         pass
 
-    invert(a, panel, (r.second, nothing, nothing, r.third, nothing, nothing, nothing, nothing))
+
+    def second():
+        r.second()
+        r.relay(0)
+
+    def third():
+        r.third()
+        r.relay(1)
+        r.relay(2)
+
+    def fourth():
+        r.relay(3)
+
+    invert(a, panel, (second, nothing, nothing, third, nothing, fourth, nothing, nothing))
 
     rows = lax.broadcasted_iota(jnp.int32, (ROWS, POINTS), 0) + sib * ROWS
     chosen = select_rows(jnp.where(rows == map_ref[...], 1.0, 0.0).astype(jnp.bfloat16), a[...])
@@ -383,27 +411,35 @@
     wide = outer[pl.ds(0, POINTS), pl.ds(pl.multiple_of(sib // 2 * BLOCK, BLOCK), BLOCK)]
     wide = pltpu.roll(wide, (sib % 2) * ROWS, 1)[:, :ROWS]
     right = product(wide.T, a[...])
-    raw_ref[: 2 * ROWS] = product(jnp.concatenate([right, chosen], axis=0), outer[pl.ds(0, POINTS), :])
+    both = product(jnp.concatenate([right, chosen], axis=0), outer[pl.ds(0, POINTS), :])
+    raw_ref[:ROWS] = raw_ref[:ROWS] - both[:ROWS]
+    raw_ref[2 * ROWS :] = -both[ROWS:]
     moved = select_columns(right, shuffle[...], ((1,), (0,)))
     r.last(1)
     r.last(3)
-    raw_ref[2 * ROWS :] = product(moved, outer[pl.ds(POINTS, POINTS), :])
+    raw_ref[ROWS : 2 * ROWS] = -product(moved, outer[pl.ds(POINTS, POINTS), :])
     g.sent()
     r.sent()
 
 
-def outputs(raw_ref, ext_ref, own_ref, cross_ref, sol_ref):
-    own_ref[...] = ext_ref[...] - raw_ref[:ROWS]
-    sol_ref[...] = -raw_ref[ROWS : 2 * ROWS]
-    cross_ref[...] = -raw_ref[2 * ROWS :]
+def outputs(raw_ref, own_ref, cross_ref, sol_ref, sem):
+    copies = [
+        pltpu.make_async_copy(raw_ref.at[pl.ds(n * ROWS, ROWS), :], out, sem.at[n])
+        for n, out in enumerate((own_ref, cross_ref, sol_ref))
+    ]
+    for copy in copies:
+        copy.start()
+    for copy in copies:
+        copy.wait()
 
 
 def on_device(t_int, t_ext, iface_map):
     vmem = pl.BlockSpec(memory_space=pltpu.VMEM)
+    anywhere = pl.BlockSpec(memory_space=pl.ANY)
     raw = pl.pallas_call(
         kernel,
-        out_shape=jax.ShapeDtypeStruct((3 * ROWS, POINTS), jnp.float32),
-        in_specs=[pl.BlockSpec(memory_space=pl.ANY), vmem],
+        out_shape=pltpu.VMEM((3 * ROWS, POINTS), jnp.float32),
+        in_specs=[anywhere, vmem, anywhere],
         out_specs=vmem,
         scratch_shapes=[
             pltpu.VMEM((16, 3, ROWS, BLOCK), jnp.float32),
@@ -417,12 +453,18 @@
             pltpu.SemaphoreType.DMA((2, COPIES)),
             pltpu.SemaphoreType.DMA((2, COPIES)),
             pltpu.SemaphoreType.DMA((2,)),
-            pltpu.SemaphoreType.DMA((4,)),
+            pltpu.SemaphoreType.DMA((5,)),
         ],
         compiler_params=pltpu.CompilerParams(collective_id=0, has_side_effects=True),
-    )(t_int[0], iface_map)
+    )(t_int[0], iface_map, t_ext[0])
     block = jax.ShapeDtypeStruct((ROWS, POINTS), jnp.float32)
-    outs = pl.pallas_call(outputs, out_shape=(block,) * 3, in_specs=[vmem] * 2, out_specs=(vmem,) * 3)(raw, t_ext[0])
+    outs = pl.pallas_call(
+        outputs,
+        out_shape=(block,) * 3,
+        in_specs=[vmem],
+        out_specs=(anywhere,) * 3,
+        scratch_shapes=[pltpu.SemaphoreType.DMA((3,))],
+    )(pltpu.with_memory_space_constraint(raw, pltpu.VMEM))
     return tuple(out[None] for out in outs)
 
 

time: 59.4 us -> 57.8 us (0.973)
  the two profiles are of different devices: /device:TPU:56 before, /device:TPU:24 now
where the time goes in v4:
time: 57.8 us; the launch traced here: 57.7 us
  Pallas kernels  56.9 us (98%)
  between operations  0.8 us (1%)
    pallas_call x1, Pallas kernels, on_device(): pl.pallas_call(kernel, out_shape=pltpu.VMEM((3 * ROWS, POINTS), jnp.float...  56.1 us

profile of v4, /device:TPU:24, one launch (start us, length us, event | category | flops | bytes accessed | tf_op | source)
XLA Modules:
  0.0 57.7 jit_solution(7028021494880572803)
XLA Ops:
  0.6 56.1 %shard_map.58.raw_ref = f32[192,512]{1,0:T(8,128)S(1)} custom-call(f32[64,1024]{1,0:T(8,128)} %bitcast.5, s32[1,512]{1,0:T(1,128)} %map_ref.1, f32[64,512]{1,0:T(8,128)} %bitcast.6), custom_call_target="tpu_custom_call" | custom-call | tf_op jit(solution)/shard_map/pallas_call | solution.py:439
  56.8 0.8 %shard_map.59 = (f32[64,512]{1,0:T(8,128)}, f32[64,512]{1,0:T(8,128)}, f32[64,512]{1,0:T(8,128)}) custom-call(f32[192,512]{1,0:T(8,128)S(1)} %shard_map.58.raw_ref), custom_call_target="tpu_custom_call" | custom-call | tf_op jit(solution)/shard_map/pallas_call | solution.py:461

commit v5 on v4

--- a/solution.py
+++ b/solution.py
@@ -126,8 +126,8 @@
 
 
 class Exchange:
-    def __init__(self, own, view, send_sem, recv_sem, near, has_more, relayed):
-        self.own, self.view, self.near, self.has_more, self.relayed = own, view, near, has_more, relayed
+    def __init__(self, own, view, send_sem, recv_sem, near, has_more):
+        self.own, self.view, self.near, self.has_more = own, view, near, has_more
         self.send_sem, self.recv_sem = send_sem, recv_sem
 
     def copy(self, index, src, dst, to):
@@ -160,23 +160,13 @@
 
     def to_opposite(self, kind, c):
         x = self.near["x"]
-        if self.relayed:
-            block = self.view(kind, (x + (1 if c % 2 else 3)) % 4, c)
-            return self.copy(XO + 4 * kind + c, block, block, "left" if c % 2 else "right")
         src = self.own(c) if kind == 0 else self.view(kind, x, c)
         return self.copy(XO + 4 * kind + c, src, self.view(kind, x, c), "opposite")
 
     def along_x(self, kind, c):
         self.to_right(kind, c).start()
         self.to_left(kind, c).start()
-        if not self.relayed:
-            self.to_opposite(kind, c).start()
-
-    def relay(self, kind):
-        self.to_right(kind, 0).wait_recv()
-        self.to_opposite(kind, 0).start()
-        self.to_left(kind, 1).wait_recv()
-        self.to_opposite(kind, 1).start()
+        self.to_opposite(kind, c).start()
 
     def more(self, kind, run):
         if self.has_more is not None:
@@ -240,10 +230,8 @@
     def last(self, kind):
         def run(even, odd):
             for c in (even, odd):
-                if c % 2 or not self.relayed:
-                    self.to_right(kind, c).wait_recv()
-                if c % 2 == 0 or not self.relayed:
-                    self.to_left(kind, c).wait_recv()
+                self.to_right(kind, c).wait_recv()
+                self.to_left(kind, c).wait_recv()
                 self.to_opposite(kind, c).wait_recv()
 
         run(0, 1)
@@ -335,8 +323,8 @@
     def row_view(kind, x, c):
         return outer.at[pl.ds(kind % 2 * POINTS + (z_of(kind) * 4 + x) * ROWS + c * HALF, HALF), :]
 
-    g = Exchange(own_tile, tile_view, send_sem.at[0], recv_sem.at[0], near, lambda kind: z_of(kind) == 0, False)
-    r = Exchange(own_rows, row_view, send_sem.at[1], recv_sem.at[1], near, None, True)
+    g = Exchange(own_tile, tile_view, send_sem.at[0], recv_sem.at[0], near, lambda kind: z_of(kind) == 0)
+    r = Exchange(own_rows, row_view, send_sem.at[1], recv_sem.at[1], near, None)
     g.first()
 
     def keep(n):
@@ -389,20 +377,7 @@
     def nothing():
         pass
 
-
-    def second():
-        r.second()
-        r.relay(0)
-
-    def third():
-        r.third()
-        r.relay(1)
-        r.relay(2)
-
-    def fourth():
-        r.relay(3)
-
-    invert(a, panel, (second, nothing, nothing, third, nothing, fourth, nothing, nothing))
+    invert(a, panel, (r.second, nothing, nothing, nothing, r.third, nothing, nothing, nothing))
 
     rows = lax.broadcasted_iota(jnp.int32, (ROWS, POINTS), 0) + sib * ROWS
     chosen = select_rows(jnp.where(rows == map_ref[...], 1.0, 0.0).astype(jnp.bfloat16), a[...])

time: 57.8 us -> 57.8 us (level)
  no operation moved by 1% of the time
where the time goes in v5:
time: 57.8 us; the launch traced here: 57.7 us
  Pallas kernels  56.9 us (98%)
  between operations  0.8 us (1%)
    pallas_call x1, Pallas kernels, on_device(): pl.pallas_call(kernel, out_shape=pltpu.VMEM((3 * ROWS, POINTS), jnp.float...  56.1 us

profile of v5, /device:TPU:24, one launch (start us, length us, event | category | flops | bytes accessed | tf_op | source)
XLA Modules:
  0.0 57.7 jit_solution(14127363131976100272)
XLA Ops:
  0.6 56.1 %shard_map.58.raw_ref = f32[192,512]{1,0:T(8,128)S(1)} custom-call(f32[64,1024]{1,0:T(8,128)} %bitcast.5, s32[1,512]{1,0:T(1,128)} %map_ref.1, f32[64,512]{1,0:T(8,128)} %bitcast.6), custom_call_target="tpu_custom_call" | custom-call | tf_op jit(solution)/shard_map/pallas_call | solution.py:414
  56.7 0.8 %shard_map.59 = (f32[64,512]{1,0:T(8,128)}, f32[64,512]{1,0:T(8,128)}, f32[64,512]{1,0:T(8,128)}) custom-call(f32[192,512]{1,0:T(8,128)S(1)} %shard_map.58.raw_ref), custom_call_target="tpu_custom_call" | custom-call | tf_op jit(solution)/shard_map/pallas_call | solution.py:436
